TPU v7x, 32 devices: a whole 2x2x4 slice. The times are simulated.
32 devices in a mesh: row: 8 (over z, x), col: 4 (over y, core).
Axes of the slice: x: 2, y: 2, z: 4, core: 2. Of those that a mesh axis runs over, the one named last changes fastest.
Arguments:
- hamiltonian: bfloat16 [2, 2048, 2048], P(None, 'row', 'col'), may hold values from -0.25 to 0.25
- basis_metric: bfloat16 [2048, 2048], P('row', 'col'), may hold values from -0.25 to 0.25
- density: bfloat16 [2, 2048, 2048], P(None, 'row', 'col'), may hold values from -6 to 6
- hamiltonian_keep: int32 [16, 16], P('row', 'col'), may hold values from 0 to 1, as said below
- metric_keep: int32 [16, 16], P('row', 'col'), may hold values from 0 to 1, as said below
- density_keep: int32 [16, 16], P('row', 'col'), may hold values from 0 to 1, as said below
- gradient_keep: int32 [16, 16], P('row', 'col'), may hold values 0 or 1
Outputs:
- gradient: float32 [2, 2048, 2048], P(None, 'row', 'col')
Inputs may be any that keep to these rules, and one draw needn't show every extreme that they name: `hamiltonian_keep`: each block row has at most 4 blocks in the pattern, and some rows have exactly 4. `metric_keep`: each block row has at most 4 blocks in the pattern, and some rows have exactly 4. `density_keep`: each block row keeps at most 7 blocks, and some rows keep exactly 7.
All inputs are finite; a program needn't handle non-finite values. No bound on the sum of `gradient_keep` on one device may be relied on, other than what follows from the above.
Results may differ from a plain program's by a relative error of at most 0.0029.
Values may be sent and summed in bfloat16 or wider, within the bound.
No kernel may reach another device: no remote copies, remote signals or barrier semaphores. Data moves between devices by JAX's collectives and lax.ppermute only.
A program may use at most 64 MiB of HBM per device.

v0:
```python
import jax
import jax.numpy as jnp
from jax import lax
from jax.sharding import PartitionSpec as P

BLOCK = 128


def widen(keep):
    return jnp.repeat(jnp.repeat(keep, BLOCK, axis=0), BLOCK, axis=1) > 0


def first_terms(rows_part, cols_part):
    hterm = jnp.einsum("srl,slc->src", rows_part[:2], cols_part, preferred_element_type=jnp.float32)
    sterm = jnp.einsum("rl,slc->src", rows_part[2], cols_part, preferred_element_type=jnp.float32)
    return jnp.concatenate([hterm, sterm], axis=0)


def second_terms(rows_part, cols_part):
    left = jnp.einsum(
        "srl,lc->src", rows_part[:2], cols_part[2], preferred_element_type=jnp.float32
    )
    right = jnp.einsum(
        "srl,slc->src", rows_part[2:], cols_part[:2], preferred_element_type=jnp.float32
    )
    return left - right


def body(
    hamiltonian, basis_metric, density, hamiltonian_keep, metric_keep, density_keep, gradient_keep
):
    kohn_sham = jnp.where(widen(hamiltonian_keep)[None], hamiltonian, jnp.zeros_like(hamiltonian))
    smat = jnp.where(widen(metric_keep), basis_metric, jnp.zeros_like(basis_metric))
    filtered = jnp.where(widen(density_keep)[None], density, jnp.zeros_like(density))
    operators = jnp.concatenate([kohn_sham, smat[None]], axis=0)
    density_cols = lax.all_gather(filtered, "row", axis=1, tiled=True)
    cols_part = density_cols
    products = first_terms(lax.all_gather(operators, "col", axis=2, tiled=True), cols_part)
    products = products.astype(jnp.bfloat16)
    operator_cols = lax.all_gather(operators, "row", axis=1, tiled=True)
    cols_part = operator_cols
    commut = second_terms(lax.all_gather(products, "col", axis=2, tiled=True), cols_part)
    grad_mask = widen(gradient_keep)[None]
    return jnp.where(grad_mask, commut, jnp.zeros_like(commut))


def solution(mesh):
    in_specs = (
        P(None, "row", "col"),
        P("row", "col"),
        P(None, "row", "col"),
        P("row", "col"),
        P("row", "col"),
        P("row", "col"),
        P("row", "col"),
    )
    out_specs = P(None, "row", "col")
    return jax.shard_map(body, mesh=mesh, in_specs=in_specs, out_specs=out_specs, check_vma=False)
```

profile of v0, /device:TPU:0, one launch (start us, length us, event | category | flops | bytes accessed | tf_op | source)
XLA Modules:
  0.0 267.1 jit_solution(11964594302407016854)
XLA Ops:
  6.5 0.0 all-gather.5.cloned.1.call-start
  6.5 0.7 broadcast_compare_fusion.2
  7.3 0.3 broadcast_in_dim.61
  7.6 0.1 copy.23
  7.7 0.7 broadcast_compare_fusion.1
  8.4 1.1 broadcast_select_fusion.1
  9.5 0.3 broadcast_in_dim.64
  9.9 1.0 fusion.6
  10.9 1.0 pad_maximum_fusion.1
  11.9 0.0 all-gather.5.cloned.1.call-update
  11.9 0.0 all-gather.7.cloned.1.call-start
  11.9 0.0 copy-done.4
  12.0 0.3 broadcast_in_dim.68
  12.3 0.1 copy.22
  12.4 0.9 broadcast_select_fusion
  13.2 0.0 all-gather.7.cloned.1.call-update
  13.3 0.0 all-gather.11.cloned.1.call-start
  13.3 0.7 all-gather.11.cloned.1.call-update
  14.0 0.0 all-gather.9.cloned.1.call-start
  14.1 29.2 %all-gather.5.cloned.1.call-done = bf16[3,256,2048]{2,1,0:T(8,128)(2,1)} async-done(((bf16[3,256,512]{2,1,0:T(8,128)(2,1)}), bf16[3,256,2048]{2,1,0:T(8,128)(2,1)}) %all-gather.5.cloned.1.call-update) | async-done | bytes 3145744 | tf_op jit(solution)/shard_map/all_gather | solution.py:38
  43.3 75.6 %all-gather.7.cloned.1.call-done = bf16[2,2048,512]{2,1,0:T(8,128)(2,1)} async-done(((bf16[2,256,512]{2,1,0:T(8,128)(2,1)}), bf16[2,2048,512]{2,1,0:T(8,128)(2,1)}) %all-gather.7.cloned.1.call-update) | async-done | bytes 4194320 | tf_op jit(solution)/shard_map/all_gather | solution.py:36
  118.9 3.9 %fusion.5 = bf16[2,256,512]{2,1,0:T(8,128)(2,1)S(1)} fusion(bf16[2,2048,512]{2,1,0:T(8,128)(2,1)} %all-gather.7.cloned.1.call-done, bf16[3,256,2048]{2,1,0:T(8,128)(2,1)} %all-gather.5.cloned.1.call-done), kind=kOutput, calls=%fused_computation.8 | convolution fusion | flops 1074003968 | bytes 5767168 | tf_op jit(solution)/shard_map/rl,slc->src/dot_general | solution.py:15
  122.8 0.0 copy-start.5
  122.8 1.3 convolution_convert_fusion
  124.1 1.1 pad_maximum_fusion
  125.2 0.0 all-gather.9.cloned.1.call-update
  125.2 0.3 broadcast_in_dim.58
  125.6 0.1 copy.24
  125.6 92.7 %all-gather.11.cloned.1.call-done = bf16[3,2048,512]{2,1,0:T(8,128)(2,1)} async-done(((bf16[3,256,512]{2,1,0:T(8,128)(2,1)}), bf16[3,2048,512]{2,1,0:T(8,128)(2,1)}) %all-gather.11.cloned.1.call-update) | async-done | bytes 6291472 | tf_op jit(solution)/shard_map/all_gather | solution.py:40
  218.4 34.1 %all-gather.9.cloned.1.call-done = bf16[4,256,2048]{2,1,0:T(8,128)(2,1)} async-done(((bf16[4,256,512]{2,1,0:T(8,128)(2,1)}), bf16[4,256,2048]{2,1,0:T(8,128)(2,1)}) %all-gather.9.cloned.1.call-update) | async-done | bytes 4194320 | tf_op jit(solution)/shard_map/all_gather | solution.py:42
  252.5 4.2 %fusion = f32[2,256,512]{2,1,0:T(8,128)S(1)} fusion(bf16[4,256,2048]{2,1,0:T(8,128)(2,1)} %all-gather.9.cloned.1.call-done, bf16[3,2048,512]{2,1,0:T(8,128)(2,1)} %all-gather.11.cloned.1.call-done), kind=kOutput, calls=%fused_computation | convolution fusion | flops 1073741824 | bytes 9437184 | tf_op jit(solution)/shard_map/srl,slc->src/dot_general | solution.py:23
  256.7 3.8 %fusion.4 = f32[2,256,512]{2,1,0:T(8,128)} fusion(f32[2,256,512]{2,1,0:T(8,128)S(1)} %fusion, bf16[4,256,2048]{2,1,0:T(8,128)(2,1)S(1)} %copy-done.2, bf16[3,2048,512]{2,1,0:T(8,128)(2,1)} %all-gather.11.cloned.1.call-done, pred[256,512]{1,0:T(8,128)(4,1)S(1)} %bitcast.52), kind=kOutput, calls=%fused_computation.5 | convolution fusion | flops 1074266112 | bytes 8519680 | tf_op jit(solution)/shard_map/srl,lc->src/dot_general | solution.py:20
  (16 shorter events, 0.1 us)
Async XLA Ops:
  6.5 5.4 %copy-start.4 = (s32[2,4]{1,0:T(2,128)S(1)}, s32[2,4]{1,0:T(2,128)}, u32[]{:S(2)}) copy-start(s32[2,4]{1,0:T(2,128)} %param.12) | copy-start | bytes 100
  6.5 5.9 %copy-start = (bf16[2,256,512]{2,1,0:T(8,128)(2,1)S(1)}, bf16[2,256,512]{2,1,0:T(8,128)(2,1)}, u32[]{:S(2)}) copy-start(bf16[2,256,512]{2,1,0:T(8,128)(2,1)} %param.9) | copy-start | bytes 1572868
  6.5 36.7 %all-gather.5.cloned.1.call-start = ((), (), s32[]{:S(2)}) async-start(), calls=%async_computation | async-start | bytes 3932160 | tf_op jit(solution)/shard_map/all_gather | solution.py:38
  11.9 107.0 %all-gather.7.cloned.1.call-start = ((), (), s32[]{:S(2)}) async-start(), calls=%async_computation.1 | async-start | bytes 4718592 | tf_op jit(solution)/shard_map/all_gather | solution.py:36
  13.3 205.1 %all-gather.11.cloned.1.call-start = ((), (), s32[]{:S(2)}) async-start(), calls=%async_computation.3 | async-start | bytes 7077888 | tf_op jit(solution)/shard_map/all_gather | solution.py:40
  14.0 238.5 %all-gather.9.cloned.1.call-start = ((), (), s32[]{:S(2)}) async-start(), calls=%async_computation.2 | async-start | bytes 5242880 | tf_op jit(solution)/shard_map/all_gather | solution.py:42
  43.3 79.5 %copy-start.3 = (bf16[3,256,2048]{2,1,0:T(8,128)(2,1)S(1)}, bf16[3,256,2048]{2,1,0:T(8,128)(2,1)}, u32[]{:S(2)}) copy-start(bf16[3,256,2048]{2,1,0:T(8,128)(2,1)} %all-gather.5.cloned.1.call-done) | copy-start | bytes 9437188
  118.9 3.9 %copy-start.1 = (bf16[2,2048,512]{2,1,0:T(8,128)(2,1)S(1)}, bf16[2,2048,512]{2,1,0:T(8,128)(2,1)}, u32[]{:S(2)}) copy-start(bf16[2,2048,512]{2,1,0:T(8,128)(2,1)} %all-gather.7.cloned.1.call-done) | copy-start | bytes 12582916
  122.8 2.4 copy-start.5
  252.5 4.2 %copy-start.2 = (bf16[4,256,2048]{2,1,0:T(8,128)(2,1)S(1)}, bf16[4,256,2048]{2,1,0:T(8,128)(2,1)}, u32[]{:S(2)}) copy-start(bf16[4,256,2048]{2,1,0:T(8,128)(2,1)} %all-gather.9.cloned.1.call-done) | copy-start | bytes 12582916
Sparse Core Ops, SparseCore 0:
  12.0 31.2 all-gather.4
  45.5 73.3 all-gather.6
  121.0 97.2 all-gather.10
  219.8 32.6 all-gather.8
where the time goes:
time: 267 us
  waiting for transfers between devices  232 us (87%)
  matrix products  13.3 us (5%)
  between operations  13.3 us (5%)
  other arithmetic  6.44 us (2%)
    all_gather x1, waiting for transfers between devices, body(): operator_cols = lax.all_gather(operators, 'row', axis=1, tiled=True)  92.7 us
    all_gather x1, waiting for transfers between devices, body(): density_cols = lax.all_gather(filtered, 'row', axis=1, tiled=True)  75.6 us
    all_gather x1, waiting for transfers between devices, body(): lax.all_gather(products, 'col', axis=2, tiled=True)  34.1 us
    all_gather x1, waiting for transfers between devices, body(): lax.all_gather(operators, 'col', axis=2, tiled=True)  29.2 us
  transfers between devices with their start and end apart: 4, of which 4 were waited for; matrix products, arithmetic and copies ran while one was open for 3% of the time, Pallas kernels for 0%

commit v1 on v0

--- a/solution.py
+++ b/solution.py
@@ -33,7 +33,13 @@
     smat = jnp.where(widen(metric_keep), basis_metric, jnp.zeros_like(basis_metric))
     filtered = jnp.where(widen(density_keep)[None], density, jnp.zeros_like(density))
     operators = jnp.concatenate([kohn_sham, smat[None]], axis=0)
-    density_cols = lax.all_gather(filtered, "row", axis=1, tiled=True)
+    size = lax.axis_size("row")
+    moving, blocks = (filtered, [filtered])
+    for _ in range(size - 1):
+        moving = lax.ppermute(moving, "row", [(i, (i + 1) % size) for i in range(size)])
+        blocks.insert(0, moving)
+    line = jnp.concatenate(blocks, axis=1)
+    density_cols = jnp.roll(line, (lax.axis_index("row") + 1) * filtered.shape[1], axis=1)
     cols_part = density_cols
     products = first_terms(lax.all_gather(operators, "col", axis=2, tiled=True), cols_part)
     products = products.astype(jnp.bfloat16)

time: 267 us -> 283 us (1.060)
  local copies, waits for them, and re-layouts: 1.63 us -> 17.4 us
  waiting for transfers between devices: 232 us -> 223 us
  starting transfers between devices: 0.12 us -> 3.09 us
    ppermute x0 -> x7, waiting for transfers between devices: none -> 91.7 us  [body(): lax.ppermute(moving, 'row', [(i, (i + 1) % size) for i in range(size)])]
    all_gather x1 -> x0, waiting for transfers between devices: 75.6 us -> none  [body(): density_cols = lax.all_gather(filtered, 'row', axis=1, tiled=True)]
    all_gather x1, waiting for transfers between devices: 29.2 us -> 0.01 us  [body(): lax.all_gather(operators, 'col', axis=2, tiled=True)]
    unnamed x15 -> x23, local copies, waits for them, and re-layouts: 0.23 us -> 16 us
    all_gather x1, waiting for transfers between devices: 92.7 us -> 101 us  [body(): operator_cols = lax.all_gather(operators, 'row', axis=1, tiled=True)]
    all_gather x1, waiting for transfers between devices: 34.1 us -> 29.8 us  [body(): lax.all_gather(products, 'col', axis=2, tiled=True)]
    ppermute x0 -> x7, starting transfers between devices: none -> 3.01 us  [body(): lax.ppermute(moving, 'row', [(i, (i + 1) % size) for i in range(size)])]
  transfers between devices with their start and end apart: 4 -> 10, of which waited for: 4 -> 9; matrix products, arithmetic and copies ran while one was open for 3% -> 8% of each run, Pallas kernels for 0% -> 0%
where the time goes in v1:
time: 283 us; the launch traced here: 282 us
  waiting for transfers between devices  223 us (79%)
  local copies, waits for them, and re-layouts  17.4 us (6%)
  matrix products  15.9 us (6%)
  between operations  13.2 us (5%)
  other arithmetic  9.26 us (3%)
  starting transfers between devices  3.09 us (1%)
    all_gather x1, waiting for transfers between devices, body(): operator_cols = lax.all_gather(operators, 'row', axis=1, tiled=True)  101 us
    ppermute x7, waiting for transfers between devices, body(): lax.ppermute(moving, 'row', [(i, (i + 1) % size) for i in range(size)])  91.7 us
    all_gather x1, waiting for transfers between devices, body(): lax.all_gather(products, 'col', axis=2, tiled=True)  29.8 us
    unnamed x23, local copies, waits for them, and re-layouts  16 us
  transfers between devices with their start and end apart: 10, of which 9 were waited for; matrix products, arithmetic and copies ran while one was open for 8% of the time, Pallas kernels for 0%

profile of v1, /device:TPU:0, one launch (start us, length us, event | category | flops | bytes accessed | tf_op | source)
XLA Modules:
  0.0 282.3 jit_solution(7701067807290225650)
XLA Ops:
  7.7 1.1 broadcast_select_fusion
  8.8 3.0 %collective-permute-start = (bf16[2,256,512]{2,1,0:T(8,128)(2,1)S(1)}, bf16[2,256,512]{2,1,0:T(8,128)(2,1)S(1)}, u32[]{:S(2)}, u32[]{:S(2)}) collective-permute-start(bf16[2,256,512]{2,1,0:T(8,128)(2,1)S(1)} %broadcast_select_fusion), channel_id=1, source_target_pairs={{0,4},{4,8},{8,12},{12,16},{16,20},{20,24},{24,28},{28,0},{1,5},{5... | collective-permute-start | bytes 1572872 | tf_op jit(solution)/shard_map/ppermute | solution.py:39
  11.8 15.0 %collective-permute-done = bf16[2,256,512]{2,1,0:T(8,128)(2,1)S(1)} collective-permute-done((bf16[2,256,512]{2,1,0:T(8,128)(2,1)S(1)}, bf16[2,256,512]{2,1,0:T(8,128)(2,1)S(1)}, u32[]{:S(2)}, u32[]{:S(2)}) %collective-permute-start) | collective-permute-done | bytes 524320 | tf_op jit(solution)/shard_map/ppermute | solution.py:39
  28.6 1.1 broadcast_select_fusion.1
  29.7 12.9 %collective-permute-done.1 = bf16[2,256,512]{2,1,0:T(8,128)(2,1)S(1)} collective-permute-done((bf16[2,256,512]{2,1,0:T(8,128)(2,1)S(1)}, bf16[2,256,512]{2,1,0:T(8,128)(2,1)S(1)}, u32[]{:S(2)}, u32[]{:S(2)}) %collective-permute-start.1) | collective-permute-done | bytes 524320 | tf_op jit(solution)/shard_map/ppermute | solution.py:39
  42.9 1.0 fusion.18
  44.0 1.0 pad_maximum_fusion.1
  45.0 12.5 %collective-permute-done.2 = bf16[2,256,512]{2,1,0:T(8,128)(2,1)S(1)} collective-permute-done((bf16[2,256,512]{2,1,0:T(8,128)(2,1)S(1)}, bf16[2,256,512]{2,1,0:T(8,128)(2,1)S(1)}, u32[]{:S(2)}, u32[]{:S(2)}) %collective-permute-start.2) | collective-permute-done | bytes 524320 | tf_op jit(solution)/shard_map/ppermute | solution.py:39
  57.5 14.0 %collective-permute-done.3 = bf16[2,256,512]{2,1,0:T(8,128)(2,1)S(1)} collective-permute-done((bf16[2,256,512]{2,1,0:T(8,128)(2,1)S(1)}, bf16[2,256,512]{2,1,0:T(8,128)(2,1)S(1)}, u32[]{:S(2)}, u32[]{:S(2)}) %collective-permute-start.3) | collective-permute-done | bytes 524320 | tf_op jit(solution)/shard_map/ppermute | solution.py:39
  71.4 13.0 %collective-permute-done.4 = bf16[2,256,512]{2,1,0:T(8,128)(2,1)S(1)} collective-permute-done((bf16[2,256,512]{2,1,0:T(8,128)(2,1)S(1)}, bf16[2,256,512]{2,1,0:T(8,128)(2,1)S(1)}, u32[]{:S(2)}, u32[]{:S(2)}) %collective-permute-start.4) | collective-permute-done | bytes 524320 | tf_op jit(solution)/shard_map/ppermute | solution.py:39
  84.5 12.2 %collective-permute-done.5 = bf16[2,256,512]{2,1,0:T(8,128)(2,1)} collective-permute-done((bf16[2,256,512]{2,1,0:T(8,128)(2,1)S(1)}, bf16[2,256,512]{2,1,0:T(8,128)(2,1)}, u32[]{:S(2)}, u32[]{:S(2)}) %collective-permute-start.5) | collective-permute-done | bytes 524320 | tf_op jit(solution)/shard_map/ppermute | solution.py:39
  96.7 12.2 %collective-permute-done.6 = bf16[2,256,512]{2,1,0:T(8,128)(2,1)} collective-permute-done((bf16[2,256,512]{2,1,0:T(8,128)(2,1)}, bf16[2,256,512]{2,1,0:T(8,128)(2,1)}, u32[]{:S(2)}, u32[]{:S(2)}) %collective-permute-start.6) | collective-permute-done | bytes 524320 | tf_op jit(solution)/shard_map/ppermute | solution.py:39
  108.9 1.9 constant_dynamic-update-slice_fusion.15
  110.8 1.8 constant_dynamic-update-slice_fusion.14
  113.4 0.8 constant_dynamic-update-slice_fusion.12
  114.3 0.8 constant_dynamic-update-slice_fusion.11
  115.1 0.8 constant_dynamic-update-slice_fusion.10
  115.9 0.8 constant_dynamic-update-slice_fusion.9
  116.8 0.9 constant_dynamic-update-slice_fusion.8
  117.7 1.9 constant_dynamic-update-slice_fusion.7
  119.6 1.9 constant_dynamic-update-slice_fusion.6
  121.4 0.8 constant_dynamic-update-slice_fusion.5
  123.9 0.8 constant_dynamic-update-slice_fusion.2
  124.7 0.9 constant_dynamic-update-slice_fusion.1
  125.6 1.0 constant_dynamic-update-slice_fusion
  126.6 4.1 %fusion.9 = bf16[2,256,512]{2,1,0:T(8,128)(2,1)S(1)} fusion(bf16[3,256,2048]{2,1,0:T(8,128)(2,1)} %all-gather.4.cloned.1.call-done, bf16[2,4096,512]{2,1,0:T(8,128)(2,1)} %constant_dynamic-update-slice_fusion, s32[]{:T(128)S(6)} %select_n.32), kind=kOutput, calls=%fused_computation.10 | convolution fusion | flops 1074003968 | bytes 7864324 | tf_op jit(solution)/shard_map/srl,slc->src/dot_general | solution.py:14
  130.7 3.8 %fusion.15 = bf16[2,256,512]{2,1,0:T(8,128)(2,1)S(1)} fusion(bf16[2,4096,512]{2,1,0:T(8,128)(2,1)} %constant_dynamic-update-slice_fusion, s32[]{:T(128)S(6)} %select_n.32, bf16[3,256,2048]{2,1,0:T(8,128)(2,1)} %all-gather.4.cloned.1.call-done), kind=kOutput, calls=%fused_computation.12 | convolution fusion | flops 1074003968 | bytes 5767172 | tf_op jit(solution)/shard_map/rl,slc->src/dot_general | solution.py:15
  134.4 1.1 pad_maximum_fusion
  136.7 29.8 %all-gather.6.cloned.1.call-done = bf16[4,256,2048]{2,1,0:T(8,128)(2,1)} async-done(((bf16[4,256,512]{2,1,0:T(8,128)(2,1)}), bf16[4,256,2048]{2,1,0:T(8,128)(2,1)}) %all-gather.6.cloned.1.call-update) | async-done | bytes 4194320 | tf_op jit(solution)/shard_map/all_gather | solution.py:48
  166.5 101.2 %all-gather.8.cloned.1.call-done = bf16[3,2048,512]{2,1,0:T(8,128)(2,1)} async-done(((bf16[3,256,512]{2,1,0:T(8,128)(2,1)}), bf16[3,2048,512]{2,1,0:T(8,128)(2,1)}) %all-gather.8.cloned.1.call-update) | async-done | bytes 6291472 | tf_op jit(solution)/shard_map/all_gather | solution.py:46
  267.7 4.2 %fusion = f32[2,256,512]{2,1,0:T(8,128)S(1)} fusion(bf16[4,256,2048]{2,1,0:T(8,128)(2,1)} %all-gather.6.cloned.1.call-done, bf16[3,2048,512]{2,1,0:T(8,128)(2,1)} %all-gather.8.cloned.1.call-done), kind=kOutput, calls=%fused_computation | convolution fusion | flops 1073741824 | bytes 9437184 | tf_op jit(solution)/shard_map/srl,slc->src/dot_general | solution.py:23
  271.9 3.8 %fusion.8 = f32[2,256,512]{2,1,0:T(8,128)} fusion(f32[2,256,512]{2,1,0:T(8,128)S(1)} %fusion, bf16[4,256,2048]{2,1,0:T(8,128)(2,1)S(1)} %copy-done.1, bf16[3,2048,512]{2,1,0:T(8,128)(2,1)} %all-gather.8.cloned.1.call-done, pred[256,512]{1,0:T(8,128)(4,1)S(1)} %bitcast.52), kind=kOutput, calls=%fused_computation.9 | convolution fusion | flops 1074266112 | bytes 8519680 | tf_op jit(solution)/shard_map/srl,lc->src/dot_general | solution.py:20
  (37 shorter events, 7.0 us)
Async XLA Ops:
  6.5 110.2 %copy-start = (bf16[2,256,512]{2,1,0:T(8,128)(2,1)S(1)}, bf16[2,256,512]{2,1,0:T(8,128)(2,1)}, u32[]{:S(2)}) copy-start(bf16[2,256,512]{2,1,0:T(8,128)(2,1)} %param.9) | copy-start | bytes 1572868
  6.5 120.0 %all-gather.4.cloned.1.call-start = ((), (), s32[]{:S(2)}) async-start(), calls=%async_computation | async-start | bytes 3932160 | tf_op jit(solution)/shard_map/all_gather | solution.py:44
  8.8 18.0 %collective-permute-start = (bf16[2,256,512]{2,1,0:T(8,128)(2,1)S(1)}, bf16[2,256,512]{2,1,0:T(8,128)(2,1)S(1)}, u32[]{:S(2)}, u32[]{:S(2)}) collective-permute-start(bf16[2,256,512]{2,1,0:T(8,128)(2,1)S(1)} %broadcast_select_fusion), channel_id=1, source_target_pairs={{0,4},{4,8},{8,12},{12,16},{16,20},{20,24},{24,28},{28,0},{1,5},{5... | collective-permute-start | bytes 1572872 | tf_op jit(solution)/shard_map/ppermute | solution.py:39
  26.8 15.8 %collective-permute-start.1 = (bf16[2,256,512]{2,1,0:T(8,128)(2,1)S(1)}, bf16[2,256,512]{2,1,0:T(8,128)(2,1)S(1)}, u32[]{:S(2)}, u32[]{:S(2)}) collective-permute-start(bf16[2,256,512]{2,1,0:T(8,128)(2,1)S(1)} %collective-permute-done), channel_id=1, source_target_pairs={{0,4},{4,8},{8,12},{12,16},{16,20},{20,24},{24,28},{28,0},{1,5},{5... | collective-permute-start | bytes 1572872 | tf_op jit(solution)/shard_map/ppermute | solution.py:39
  42.6 14.9 %collective-permute-start.2 = (bf16[2,256,512]{2,1,0:T(8,128)(2,1)S(1)}, bf16[2,256,512]{2,1,0:T(8,128)(2,1)S(1)}, u32[]{:S(2)}, u32[]{:S(2)}) collective-permute-start(bf16[2,256,512]{2,1,0:T(8,128)(2,1)S(1)} %collective-permute-done.1), channel_id=1, source_target_pairs={{0,4},{4,8},{8,12},{12,16},{16,20},{20,24},{24,28},{28,0},{1,5},{5... | collective-permute-start | bytes 1572872 | tf_op jit(solution)/shard_map/ppermute | solution.py:39
  45.0 121.5 %all-gather.6.cloned.1.call-start = ((), (), s32[]{:S(2)}) async-start(), calls=%async_computation.1 | async-start | bytes 5242880 | tf_op jit(solution)/shard_map/all_gather | solution.py:48
  57.5 14.0 %collective-permute-start.3 = (bf16[2,256,512]{2,1,0:T(8,128)(2,1)S(1)}, bf16[2,256,512]{2,1,0:T(8,128)(2,1)S(1)}, u32[]{:S(2)}, u32[]{:S(2)}) collective-permute-start(bf16[2,256,512]{2,1,0:T(8,128)(2,1)S(1)} %collective-permute-done.2), channel_id=1, source_target_pairs={{0,4},{4,8},{8,12},{12,16},{16,20},{20,24},{24,28},{28,0},{1,5},{5... | collective-permute-start | bytes 1572872 | tf_op jit(solution)/shard_map/ppermute | solution.py:39
  71.4 13.0 %collective-permute-start.4 = (bf16[2,256,512]{2,1,0:T(8,128)(2,1)S(1)}, bf16[2,256,512]{2,1,0:T(8,128)(2,1)S(1)}, u32[]{:S(2)}, u32[]{:S(2)}) collective-permute-start(bf16[2,256,512]{2,1,0:T(8,128)(2,1)S(1)} %collective-permute-done.3), channel_id=1, source_target_pairs={{0,4},{4,8},{8,12},{12,16},{16,20},{20,24},{24,28},{28,0},{1,5},{5... | collective-permute-start | bytes 1572872 | tf_op jit(solution)/shard_map/ppermute | solution.py:39
  84.5 12.2 %collective-permute-start.5 = (bf16[2,256,512]{2,1,0:T(8,128)(2,1)S(1)}, bf16[2,256,512]{2,1,0:T(8,128)(2,1)}, u32[]{:S(2)}, u32[]{:S(2)}) collective-permute-start(bf16[2,256,512]{2,1,0:T(8,128)(2,1)S(1)} %collective-permute-done.4), channel_id=1, source_target_pairs={{0,4},{4,8},{8,12},{12,16},{16,20},{20,24},{24,28},{28,0},{1,5},{5... | collective-permute-start | bytes 1572872 | tf_op jit(solution)/shard_map/ppermute | solution.py:39
  96.7 12.2 %collective-permute-start.6 = (bf16[2,256,512]{2,1,0:T(8,128)(2,1)}, bf16[2,256,512]{2,1,0:T(8,128)(2,1)}, u32[]{:S(2)}, u32[]{:S(2)}) collective-permute-start(bf16[2,256,512]{2,1,0:T(8,128)(2,1)} %collective-permute-done.5), channel_id=1, source_target_pairs={{0,4},{4,8},{8,12},{12,16},{16,20},{20,24},{24,28},{28,0},{1,5},{5... | collective-permute-start | bytes 1572872 | tf_op jit(solution)/shard_map/ppermute | solution.py:39
  130.6 5.6 %copy-start.2 = (s32[2,4]{1,0:T(2,128)S(1)}, s32[2,4]{1,0:T(2,128)}, u32[]{:S(2)}) copy-start(s32[2,4]{1,0:T(2,128)} %param.13) | copy-start | bytes 100
  135.5 132.2 %all-gather.8.cloned.1.call-start = ((), (), s32[]{:S(2)}) async-start(), calls=%async_computation.2 | async-start | bytes 7077888 | tf_op jit(solution)/shard_map/all_gather | solution.py:46
  267.7 4.2 %copy-start.1 = (bf16[4,256,2048]{2,1,0:T(8,128)(2,1)S(1)}, bf16[4,256,2048]{2,1,0:T(8,128)(2,1)}, u32[]{:S(2)}) copy-start(bf16[4,256,2048]{2,1,0:T(8,128)(2,1)} %all-gather.6.cloned.1.call-done) | copy-start | bytes 12582916
Sparse Core Ops, SparseCore 0:
  45.1 29.7 all-gather.3
  135.6 30.7 all-gather.5
  168.7 99.0 all-gather.7
